TPU v7x, 32 devices: a whole 2x2x4 slice. The times are simulated.
32 devices in a mesh: cp: 4 (over y, x), fsdp: 2 (over core), rep: 4 (over z).
Axes of the slice: x: 2, y: 2, z: 4, core: 2. Of those that a mesh axis runs over, the one named last changes fastest.
Arguments:
- tokens: bfloat16 [16, 2048, 768], P(('fsdp', 'rep'), 'cp'), may hold values from -6 to 6
- segments: int32 [16, 2048], P(('fsdp', 'rep')), may hold values from 0 to 3, never falling along the last dimension, each value on 1 to 1024 neighbouring positions
- g_one: bfloat16 [768], P('fsdp'), may hold values from 0.099609375 to 1.8984375
- b_one: bfloat16 [768], P('fsdp'), may hold values from -3 to 3
- w_qkv: bfloat16 [768, 2304], P('fsdp'), may hold values from -0.21875 to 0.21875
- b_query: bfloat16 [768], P('fsdp'), may hold values from -3 to 3
- b_value: bfloat16 [768], P('fsdp'), may hold values from -3 to 3
- w_out: bfloat16 [768, 768], P('fsdp'), may hold values from -1.75 to 1.75
- b_out: bfloat16 [768], P('fsdp'), may hold values from -3 to 3
- g_two: bfloat16 [768], P('fsdp'), may hold values from 0.099609375 to 1.8984375
- b_two: bfloat16 [768], P('fsdp'), may hold values from -3 to 3
- w_fc: bfloat16 [768, 3072], P('fsdp'), may hold values from -0.21875 to 0.21875
- b_fc: bfloat16 [3072], P('fsdp'), may hold values from -3 to 3
- w_proj: bfloat16 [3072, 768], P('fsdp'), may hold values from -0.109375 to 0.109375
- b_proj: bfloat16 [768], P('fsdp'), may hold values from -3 to 3
- cotangent: bfloat16 [16, 2048, 768], P(('fsdp', 'rep'), 'cp'), may hold values from -6 to 6
Outputs:
- layer_out: bfloat16 [16, 2048, 768], P(('fsdp', 'rep'), 'cp')
- tokens_grad: bfloat16 [16, 2048, 768], P(('fsdp', 'rep'), 'cp')
- dg_one: float32 [768], P('fsdp')
- db_one: float32 [768], P('fsdp')
- dw_qkv: float32 [768, 2304], P('fsdp')
- db_query: float32 [768], P('fsdp')
- db_value: float32 [768], P('fsdp')
- dw_out: float32 [768, 768], P('fsdp')
- db_out: float32 [768], P('fsdp')
- dg_two: float32 [768], P('fsdp')
- db_two: float32 [768], P('fsdp')
- dw_fc: float32 [768, 3072], P('fsdp')
- db_fc: float32 [3072], P('fsdp')
- dw_proj: float32 [3072, 768], P('fsdp')
- db_proj: float32 [768], P('fsdp')
Inputs may be any that keep to these rules, and one draw needn't show every extreme that they name: `segments`: in each sequence the ids never fall, and each document holds 1 to 1024 positions, one document exactly that many.
All inputs are finite; a program needn't handle non-finite values.
Results may differ from a plain program's by a relative error of at most 0.012.
The roundings to bfloat16 on the way count: a program that leaves them out, or rounds other values in their place, can miss the bound.
Values may be sent and summed in bfloat16 or wider, within the bound.
A program may use at most 384 MiB of HBM per device.

v0:
```python
import jax
import jax.numpy as jnp
from jax import lax
from jax.sharding import PartitionSpec as P

HEADS = 12


def layer_norm(value, gain, shift):
    center = value - jnp.mean(value, axis=-1, keepdims=True)
    spread = jnp.mean(center * center, axis=-1, keepdims=True)
    return center * lax.rsqrt(spread + 1e-05) * gain + shift


def gelu_tanh(value):
    return (
        0.5
        * value
        * (1.0 + jnp.tanh(0.7978845608028654 * (value + 0.044715 * value * value * value)))
    )


def inner_rows(left, right):
    return lax.dot_general(
        left, right, (((0,), (0,)), ((), ())), preferred_element_type=jnp.float32
    )


def times_trans(left, right):
    return lax.dot_general(
        left, right, (((1,), (1,)), ((), ())), preferred_element_type=jnp.float32
    )


def body(
    tokens,
    segments,
    g_one,
    b_one,
    w_qkv,
    b_query,
    b_value,
    w_out,
    b_out,
    g_two,
    b_two,
    w_fc,
    b_fc,
    w_proj,
    b_proj,
    cotangent,
):
    seqs, span, width = tokens.shape
    seq_len = segments.shape[1]
    rows = seqs * span
    size = width // HEADS
    scale = size ** (-0.5)
    first_pos = lax.axis_index("cp") * span
    full = (
        lax.all_gather(g_one, "fsdp", axis=0, tiled=True),
        lax.all_gather(b_one, "fsdp", axis=0, tiled=True),
        lax.all_gather(w_qkv, "fsdp", axis=0, tiled=True),
        lax.all_gather(b_query, "fsdp", axis=0, tiled=True),
        lax.all_gather(b_value, "fsdp", axis=0, tiled=True),
        lax.all_gather(w_out, "fsdp", axis=0, tiled=True),
        lax.all_gather(b_out, "fsdp", axis=0, tiled=True),
        lax.all_gather(g_two, "fsdp", axis=0, tiled=True),
        lax.all_gather(b_two, "fsdp", axis=0, tiled=True),
        lax.all_gather(w_fc, "fsdp", axis=0, tiled=True),
        lax.all_gather(b_fc, "fsdp", axis=0, tiled=True),
        lax.all_gather(w_proj, "fsdp", axis=0, tiled=True),
        lax.all_gather(b_proj, "fsdp", axis=0, tiled=True),
    )
    gain_one = full[0].astype(jnp.float32)
    shift_one = full[1].astype(jnp.float32)
    gain_two = full[7].astype(jnp.float32)
    shift_two = full[8].astype(jnp.float32)
    tok_rows = tokens.reshape(rows, width).astype(jnp.float32)
    normed = layer_norm(tok_rows, gain_one, shift_one).astype(jnp.bfloat16)
    qkv_bias = jnp.concatenate([full[3], jnp.zeros_like(full[3]), full[4]]).astype(jnp.float32)
    merged = (jnp.dot(normed, full[2], preferred_element_type=jnp.float32) + qkv_bias).astype(
        jnp.bfloat16
    )
    merged = merged.reshape(seqs, span, 3 * width)
    query = merged[:, :, :width]
    key_loc = merged[:, :, width : 2 * width]
    value_loc = merged[:, :, 2 * width :]
    keys_all, values_all = (
        lax.all_gather(key_loc, "cp", axis=1, tiled=True),
        lax.all_gather(value_loc, "cp", axis=1, tiled=True),
    )
    key_pos = jnp.arange(seq_len)

    def masked_scores(q_rows, k_rows, seq_ids, near_ids):
        length = k_rows.shape[0]
        q_three = q_rows.reshape(span, HEADS, size)
        k_three = k_rows.reshape(length, HEADS, size)
        scores = (
            jnp.einsum("qhd,khd->hqk", q_three, k_three, preferred_element_type=jnp.float32) * scale
        )
        query_ids = lax.dynamic_slice_in_dim(seq_ids, first_pos, span)
        query_pos = first_pos + jnp.arange(span)
        allowed = (query_ids[:, None] == near_ids[None, :]) & (
            key_pos[None, :] <= query_pos[:, None]
        )
        return jnp.where(allowed[None], scores, -1e30)

    def attend(item):
        q_rows, k_rows, v_rows, seq_ids, near_ids = item
        length = k_rows.shape[0]
        scores = masked_scores(q_rows, k_rows, seq_ids, near_ids)
        top = jnp.max(scores, axis=-1, keepdims=True)
        expo = jnp.exp(scores - top)
        total = jnp.sum(expo, axis=-1, keepdims=True)
        probs = (expo / total).astype(jnp.bfloat16)
        mixed = jnp.einsum(
            "hqk,khd->qhd",
            probs,
            v_rows.reshape(length, HEADS, size),
            preferred_element_type=jnp.float32,
        )
        return (
            mixed.reshape(span, width).astype(jnp.bfloat16),
            top[..., 0] + jnp.log(total[..., 0]),
        )

    mixed, log_total = lax.map(attend, (query, keys_all, values_all, segments, segments))
    mixed_rows = mixed.reshape(rows, width)
    branch = jnp.dot(mixed_rows, full[5], preferred_element_type=jnp.float32) + full[6].astype(
        jnp.float32
    )
    resid = tok_rows + branch
    normed_two = layer_norm(resid, gain_two, shift_two).astype(jnp.bfloat16)
    hidden = jnp.dot(normed_two, full[9], preferred_element_type=jnp.float32) + full[10].astype(
        jnp.float32
    )
    active = gelu_tanh(hidden).astype(jnp.bfloat16)
    output = jnp.dot(active, full[11], preferred_element_type=jnp.float32) + full[12].astype(
        jnp.float32
    )
    layer_out = (resid + output).astype(jnp.bfloat16).reshape(seqs, span, width)
    back = (
        lax.all_gather(g_one, "fsdp", axis=0, tiled=True),
        lax.all_gather(b_one, "fsdp", axis=0, tiled=True),
        lax.all_gather(w_qkv, "fsdp", axis=0, tiled=True),
        lax.all_gather(b_query, "fsdp", axis=0, tiled=True),
        lax.all_gather(b_value, "fsdp", axis=0, tiled=True),
        lax.all_gather(w_out, "fsdp", axis=0, tiled=True),
        lax.all_gather(b_out, "fsdp", axis=0, tiled=True),
        lax.all_gather(g_two, "fsdp", axis=0, tiled=True),
        lax.all_gather(b_two, "fsdp", axis=0, tiled=True),
        lax.all_gather(w_fc, "fsdp", axis=0, tiled=True),
        lax.all_gather(b_fc, "fsdp", axis=0, tiled=True),
        lax.all_gather(w_proj, "fsdp", axis=0, tiled=True),
        lax.all_gather(b_proj, "fsdp", axis=0, tiled=True),
    )
    keys_b, values_b = (
        lax.all_gather(key_loc, "cp", axis=1, tiled=True),
        lax.all_gather(value_loc, "cp", axis=1, tiled=True),
    )
    out_grad = cotangent.reshape(rows, width).astype(jnp.float32)
    d_output = out_grad.astype(jnp.bfloat16)
    dw_proj = inner_rows(active, d_output)
    db_proj = jnp.sum(d_output.astype(jnp.float32), axis=0)
    d_active = times_trans(d_output, back[11])
    _, gelu_pull = jax.vjp(gelu_tanh, hidden)
    d_hidden = gelu_pull(d_active)[0].astype(jnp.bfloat16)
    dw_fc = inner_rows(normed_two, d_hidden)
    db_fc = jnp.sum(d_hidden.astype(jnp.float32), axis=0)
    d_normed_two = times_trans(d_hidden, back[9])
    _, norm_pull_two = jax.vjp(
        layer_norm, resid, back[7].astype(jnp.float32), back[8].astype(jnp.float32)
    )
    d_resid_part, dg_two, db_two = norm_pull_two(d_normed_two)
    d_resid = out_grad + d_resid_part
    d_branch = d_resid.astype(jnp.bfloat16)
    dw_out = inner_rows(mixed_rows, d_branch)
    db_out = jnp.sum(d_branch.astype(jnp.float32), axis=0)
    d_mixed = times_trans(d_branch, back[5]).astype(jnp.bfloat16).reshape(seqs, span, width)

    def attend_back(item):
        q_rows, k_rows, v_rows, seq_ids, near_ids, d_rows, lse_rows = item
        length = k_rows.shape[0]
        scores = masked_scores(q_rows, k_rows, seq_ids, near_ids)
        probs = jnp.exp(scores - lse_rows[..., None])
        d_three = d_rows.reshape(span, HEADS, size)
        v_three = v_rows.reshape(length, HEADS, size)
        d_probs = jnp.einsum("qhd,khd->hqk", d_three, v_three, preferred_element_type=jnp.float32)
        delta = jnp.sum(probs * d_probs, axis=-1, keepdims=True)
        d_scores = (probs * (d_probs - delta)).astype(jnp.bfloat16)
        d_query = (
            jnp.einsum(
                "hqk,khd->qhd",
                d_scores,
                k_rows.reshape(length, HEADS, size),
                preferred_element_type=jnp.float32,
            )
            * scale
        )
        d_key = (
            jnp.einsum(
                "hqk,qhd->khd",
                d_scores,
                q_rows.reshape(span, HEADS, size),
                preferred_element_type=jnp.float32,
            )
            * scale
        )
        d_value = jnp.einsum(
            "hqk,qhd->khd", probs.astype(jnp.bfloat16), d_three, preferred_element_type=jnp.float32
        )
        return (
            d_query.reshape(span, width),
            d_key.reshape(length, width),
            d_value.reshape(length, width),
        )

    d_query, d_key_all, d_value_all = lax.map(
        attend_back, (query, keys_b, values_b, segments, segments, d_mixed, log_total)
    )
    d_key, d_value = (
        lax.psum_scatter(d_key_all, "cp", scatter_dimension=1, tiled=True),
        lax.psum_scatter(d_value_all, "cp", scatter_dimension=1, tiled=True),
    )
    d_merged = (
        jnp.concatenate([d_query, d_key, d_value], axis=-1)
        .astype(jnp.bfloat16)
        .reshape(rows, 3 * width)
    )
    d_merged_f = d_merged.astype(jnp.float32)
    db_query = jnp.sum(d_merged_f[:, :width], axis=0)
    db_value = jnp.sum(d_merged_f[:, 2 * width :], axis=0)
    dw_qkv = inner_rows(normed, d_merged)
    d_normed = times_trans(d_merged, back[2])
    _, norm_pull_one = jax.vjp(
        layer_norm, tok_rows, back[0].astype(jnp.float32), back[1].astype(jnp.float32)
    )
    d_tok_part, dg_one, db_one = norm_pull_one(d_normed)
    tokens_grad = (d_resid + d_tok_part).astype(jnp.bfloat16).reshape(seqs, span, width)
    shards = (
        lax.psum_scatter(dg_one, "fsdp", scatter_dimension=0, tiled=True),
        lax.psum_scatter(db_one, "fsdp", scatter_dimension=0, tiled=True),
        lax.psum_scatter(dw_qkv, "fsdp", scatter_dimension=0, tiled=True),
        lax.psum_scatter(db_query, "fsdp", scatter_dimension=0, tiled=True),
        lax.psum_scatter(db_value, "fsdp", scatter_dimension=0, tiled=True),
        lax.psum_scatter(dw_out, "fsdp", scatter_dimension=0, tiled=True),
        lax.psum_scatter(db_out, "fsdp", scatter_dimension=0, tiled=True),
        lax.psum_scatter(dg_two, "fsdp", scatter_dimension=0, tiled=True),
        lax.psum_scatter(db_two, "fsdp", scatter_dimension=0, tiled=True),
        lax.psum_scatter(dw_fc, "fsdp", scatter_dimension=0, tiled=True),
        lax.psum_scatter(db_fc, "fsdp", scatter_dimension=0, tiled=True),
        lax.psum_scatter(dw_proj, "fsdp", scatter_dimension=0, tiled=True),
        lax.psum_scatter(db_proj, "fsdp", scatter_dimension=0, tiled=True),
    )
    totals = lax.psum(
        (
            shards[0],
            shards[1],
            shards[2],
            shards[3],
            shards[4],
            shards[5],
            shards[6],
            shards[7],
            shards[8],
            shards[9],
            shards[10],
            shards[11],
            shards[12],
        ),
        ("cp", "rep"),
    )
    return (
        layer_out,
        tokens_grad,
        totals[0],
        totals[1],
        totals[2],
        totals[3],
        totals[4],
        totals[5],
        totals[6],
        totals[7],
        totals[8],
        totals[9],
        totals[10],
        totals[11],
        totals[12],
    )


def solution(mesh):
    placed = (
        P(("fsdp", "rep"), "cp", None),
        P(("fsdp", "rep"), None),
        P("fsdp"),
        P("fsdp"),
        P("fsdp", None),
        P("fsdp"),
        P("fsdp"),
        P("fsdp", None),
        P("fsdp"),
        P("fsdp"),
        P("fsdp"),
        P("fsdp", None),
        P("fsdp"),
        P("fsdp", None),
        P("fsdp"),
        P(("fsdp", "rep"), "cp", None),
    )
    return jax.shard_map(
        body,
        mesh=mesh,
        in_specs=placed,
        out_specs=(
            P(("fsdp", "rep"), "cp", None),
            P(("fsdp", "rep"), "cp", None),
            P("fsdp"),
            P("fsdp"),
            P("fsdp", None),
            P("fsdp"),
            P("fsdp"),
            P("fsdp", None),
            P("fsdp"),
            P("fsdp"),
            P("fsdp"),
            P("fsdp", None),
            P("fsdp"),
            P("fsdp", None),
            P("fsdp"),
        ),
        check_vma=False,
    )
```

profile of v0, /device:TPU:0, one launch (start us, length us, event | category | flops | bytes accessed | tf_op | source)
XLA Modules:
  0.0 1499.2 jit_solution(1097224443274911993)
XLA Ops:
  50.4 56.1 %all-gather.20.cloned.1.call-done = bf16[2,2048,768]{1,2,0:T(8,128)(2,1)} async-done(((bf16[2,512,768]{1,2,0:T(8,128)(2,1)}), bf16[2,2048,768]{1,2,0:T(8,128)(2,1)}) %all-gather.20.cloned.1.call-update) | async-done | bytes 6291472 | tf_op jit(solution)/shard_map/all_gather | solution.py:89
  106.5 72.5 %all-gather.18.cloned.1.call-done = bf16[2,2048,768]{1,2,0:T(8,128)(2,1)} async-done(((bf16[2,512,768]{1,2,0:T(8,128)(2,1)}), bf16[2,2048,768]{1,2,0:T(8,128)(2,1)}) %all-gather.18.cloned.1.call-update) | async-done | bytes 6291472 | tf_op jit(solution)/shard_map/all_gather | solution.py:90
  178.9 155.2 %while.34 = (s32[]{:T(128)}, bf16[2,512,768]{2,1,0:T(8,128)(2,1)}, f32[2,12,512]{2,1,0:T(8,128)S(1)}, bf16[2,2048,768]{1,2,0:T(8,128)(2,1)}, s32[2,2048]{1,0:T(2...) while((s32[]{:T(128)}, bf16[2,512,768]{2,1,0:T(8,128)(2,1)}, ...), condition=%wide.region_5.6_spmd.clone, body=%wide.region_2.5_spmd.clone.sunk | while | flops 3375753728 | bytes 197388496 | solution.py:127
  188.6 23.9 %fusion.106 = (f32[12,512]{1,0:T(8,128)S(1)}, f32[12,512,2048]{2,1,0:T(8,128)}) fusion(pred[512,2048]{1,0:T(8,128)(4,1)} %fusion.105, bf16[512,12,64]{0,2,1:T(8,128)(2,1)} %bitcast.170, bf16[2048,12,64]{0,2,1:T(8,128)(2,1)S(1)} %bitcast.165), kind=kOutput, calls=%fused_computation.5.clone.1 | convolution fusion | flops 1648355328 | bytes 55336960 | tf_op jit(solution)/shard_map/while/body/eval_jaxpr/qhd,khd->hqk/dot_general | solution.py:99
  212.5 24.5 %fusion.107 = f32[12,512]{1,0:T(8,128)S(1)} fusion(f32[12,512,2048]{2,1,0:T(8,128)} %get-tuple-element.683, f32[12,512]{1,0:T(8,128)S(1)} %get-tuple-element.684, pred[512,2048]{1,0:T(8,128)(4,1)} %fusion.105), kind=kLoop, calls=%fused_computation.6.clone.1 | loop fusion | flops 50325504 | bytes 51429376 | tf_op jit(solution)/shard_map/while/body/eval_jaxpr/reduce_sum | solution.py:114
  237.1 20.2 %fusion.108 = bf16[12,64,512]{2,1,0:T(8,128)(2,1)S(1)} fusion(bf16[2048,12,64]{0,2,1:T(8,128)(2,1)S(1)} %bitcast.174, f32[12,512,2048]{2,1,0:T(8,128)} %get-tuple-element.683, f32[12,512]{1,0:T(8,128)S(1)} %fusion.107, f32[12,512]{1,0:T(8,128)S(1)} %get-tuple-element.684, pred[512,2048]{1,0:T(8,128)(4,1)S(1)} %copy-done), kind=kOutput, calls=%fused_computation.10.clone.1 | convolution fusion | flops 1673920512 | bytes 55361536 | tf_op jit(solution)/shard_map/while/body/eval_jaxpr/hqk,khd->qhd/dot_general | solution.py:116
  268.2 21.5 %fusion.106 = (f32[12,512]{1,0:T(8,128)S(1)}, f32[12,512,2048]{2,1,0:T(8,128)}) fusion(pred[512,2048]{1,0:T(8,128)(4,1)} %fusion.105, bf16[512,12,64]{0,2,1:T(8,128)(2,1)} %bitcast.170, bf16[2048,12,64]{0,2,1:T(8,128)(2,1)S(1)} %bitcast.165), kind=kOutput, calls=%fused_computation.5.clone.1 | convolution fusion | flops 1648355328 | bytes 55336960 | tf_op jit(solution)/shard_map/while/body/eval_jaxpr/qhd,khd->hqk/dot_general | solution.py:99
  289.7 22.9 %fusion.107 = f32[12,512]{1,0:T(8,128)S(1)} fusion(f32[12,512,2048]{2,1,0:T(8,128)} %get-tuple-element.683, f32[12,512]{1,0:T(8,128)S(1)} %get-tuple-element.684, pred[512,2048]{1,0:T(8,128)(4,1)} %fusion.105), kind=kLoop, calls=%fused_computation.6.clone.1 | loop fusion | flops 50325504 | bytes 51429376 | tf_op jit(solution)/shard_map/while/body/eval_jaxpr/reduce_sum | solution.py:114
  312.5 20.2 %fusion.108 = bf16[12,64,512]{2,1,0:T(8,128)(2,1)S(1)} fusion(bf16[2048,12,64]{0,2,1:T(8,128)(2,1)S(1)} %bitcast.174, f32[12,512,2048]{2,1,0:T(8,128)} %get-tuple-element.683, f32[12,512]{1,0:T(8,128)S(1)} %fusion.107, f32[12,512]{1,0:T(8,128)S(1)} %get-tuple-element.684, pred[512,2048]{1,0:T(8,128)(4,1)S(1)} %copy-done), kind=kOutput, calls=%fused_computation.10.clone.1 | convolution fusion | flops 1673920512 | bytes 55361536 | tf_op jit(solution)/shard_map/while/body/eval_jaxpr/hqk,khd->qhd/dot_general | solution.py:116
  349.5 18.8 %convert_reduce_fusion = (f32[3072]{0:T(1024)}, bf16[1024,3072]{1,0:T(8,128)(2,1)S(1)}) fusion(bf16[1024,768]{1,0:T(8,128)(2,1)} %bitcast.176, bf16[3072,768]{1,0:T(8,128)(2,1)} %all-gather.26.cloned.1.call-done, f32[1024,3072]{1,0:T(8,128)} %fusion.43, f32[3072]{0:T(1024)S(1)} %bitcast.201), kind=kOutput, calls=%fused_computation.52 | convolution fusion | flops 4916769792 | bytes 25190400 | tf_op jit(solution)/shard_map/dot_general | solution.py:30
  379.7 375.4 %while.35 = (s32[]{:T(128)}, bf16[2,512,768]{2,1,0:T(8,128)(2,1)}, f32[2,2048,768]{2,1,0:T(8,128)}, f32[2,2048,768]{2,1,0:T(8,128)}, bf16[2,2048,768]{1,2,0:T(8,...) while((s32[]{:T(128)}, bf16[2,512,768]{2,1,0:T(8,128)(2,1)}, ...), condition=%wide.region_12.13_spmd.clone, body=%wide.region_10.12_spmd.clone.sunk | while | flops 8247306752 | bytes 519514368 | solution.py:218
  392.5 20.5 %fusion.119 = f32[12,512,2048]{2,1,0:T(8,128)} fusion(bf16[512,12,64]{0,2,1:T(8,128)(2,1)} %bitcast.167, bf16[2048,12,64]{0,2,1:T(8,128)(2,1)S(1)} %bitcast.162), kind=kOutput, calls=%fused_computation.114.clone.1 | convolution fusion | flops 1610612736 | bytes 54263808 | tf_op jit(solution)/shard_map/while/body/eval_jaxpr/qhd,khd->hqk/dot_general | solution.py:99
  413.0 23.1 %fusion.121 = f32[12,64,2048]{2,1,0:T(8,128)} fusion(bf16[512,12,64]{0,2,1:T(8,128)(2,1)} %bitcast.172, f32[12,512,2048]{2,1,0:T(8,128)} %fusion.119, f32[12,512]{1,0:T(8,128)S(1)} %dynamic-slice_bitcast_fusion.2, pred[512,2048]{1,0:T(8,128)(4,1)} %fusion.120), kind=kOutput, calls=%fused_computation.24.clone.1 | convolution fusion | flops 1660944384 | bytes 58482688 | tf_op jit(solution)/shard_map/while/body/eval_jaxpr/hqk,qhd->khd/dot_general | solution.py:209
  442.7 37.6 %multiply_reduce_fusion.5 = (f32[12,512]{1,0:T(8,128)S(1)}, f32[12,512,2048]{2,1,0:T(8,128)}) fusion(f32[12,512,2048]{2,1,0:T(8,128)} %fusion.119, f32[12,512]{1,0:T(8,128)S(1)} %dynamic-slice_bitcast_fusion.2, pred[512,2048]{1,0:T(8,128)(4,1)} %fusion.120, bf16[512,12,64]{0,2,1:T(8,128)(2,1)} %bitcast.173, bf16[2048,12,64]{0,2,1:T(8,128)(2,1)} %bitcast.166), kind=kOutput, calls=%fused_computation.21.clone.1 | convolution fusion | flops 1673521152 | bytes 105693184 | tf_op jit(solution)/shard_map/while/body/eval_jaxpr/qhd,khd->hqk/dot_general | solution.py:188
  480.3 41.4 %multiply_convert_fusion.5 = bf16[12,512,2048]{2,1,0:T(8,128)(2,1)} fusion(f32[12,512,2048]{2,1,0:T(8,128)} %get-tuple-element.697, f32[12,512,2048]{2,1,0:T(8,128)} %fusion.119, f32[12,512]{1,0:T(8,128)S(1)} %get-tuple-element.698, f32[12,512]{1,0:T(8,128)S(1)} %dynamic-slice_bitcast_fusion.2, pred[512,2048]{1,0:T(8,128)(4,1)} %fusion.120), kind=kLoop, calls=%fused_computation.20.clone.1 | loop fusion | flops 75497472 | bytes 126926848 | tf_op jit(solution)/shard_map/while/body/eval_jaxpr/convert_element_type | solution.py:190
  521.7 13.4 convolution_multiply_fusion.4
  535.1 15.5 %convolution_multiply_fusion.5 = f32[12,64,2048]{2,1,0:T(8,128)} fusion(bf16[512,12,64]{0,2,1:T(8,128)(2,1)} %bitcast.168, bf16[12,512,2048]{2,1,0:T(8,128)(2,1)} %multiply_convert_fusion.5), kind=kOutput, calls=%fused_computation.28.clone.1 | convolution fusion | flops 1612185600 | bytes 32243712 | tf_op jit(solution)/shard_map/while/body/eval_jaxpr/hqk,qhd->khd/dot_general | solution.py:201
  578.6 20.5 %fusion.119 = f32[12,512,2048]{2,1,0:T(8,128)} fusion(bf16[512,12,64]{0,2,1:T(8,128)(2,1)} %bitcast.167, bf16[2048,12,64]{0,2,1:T(8,128)(2,1)S(1)} %bitcast.162), kind=kOutput, calls=%fused_computation.114.clone.1 | convolution fusion | flops 1610612736 | bytes 54263808 | tf_op jit(solution)/shard_map/while/body/eval_jaxpr/qhd,khd->hqk/dot_general | solution.py:99
  599.1 23.1 %fusion.121 = f32[12,64,2048]{2,1,0:T(8,128)} fusion(bf16[512,12,64]{0,2,1:T(8,128)(2,1)} %bitcast.172, f32[12,512,2048]{2,1,0:T(8,128)} %fusion.119, f32[12,512]{1,0:T(8,128)S(1)} %dynamic-slice_bitcast_fusion.2, pred[512,2048]{1,0:T(8,128)(4,1)} %fusion.120), kind=kOutput, calls=%fused_computation.24.clone.1 | convolution fusion | flops 1660944384 | bytes 58482688 | tf_op jit(solution)/shard_map/while/body/eval_jaxpr/hqk,qhd->khd/dot_general | solution.py:209
  628.9 37.6 %multiply_reduce_fusion.5 = (f32[12,512]{1,0:T(8,128)S(1)}, f32[12,512,2048]{2,1,0:T(8,128)}) fusion(f32[12,512,2048]{2,1,0:T(8,128)} %fusion.119, f32[12,512]{1,0:T(8,128)S(1)} %dynamic-slice_bitcast_fusion.2, pred[512,2048]{1,0:T(8,128)(4,1)} %fusion.120, bf16[512,12,64]{0,2,1:T(8,128)(2,1)} %bitcast.173, bf16[2048,12,64]{0,2,1:T(8,128)(2,1)} %bitcast.166), kind=kOutput, calls=%fused_computation.21.clone.1 | convolution fusion | flops 1673521152 | bytes 105693184 | tf_op jit(solution)/shard_map/while/body/eval_jaxpr/qhd,khd->hqk/dot_general | solution.py:188
  666.4 41.4 %multiply_convert_fusion.5 = bf16[12,512,2048]{2,1,0:T(8,128)(2,1)} fusion(f32[12,512,2048]{2,1,0:T(8,128)} %get-tuple-element.697, f32[12,512,2048]{2,1,0:T(8,128)} %fusion.119, f32[12,512]{1,0:T(8,128)S(1)} %get-tuple-element.698, f32[12,512]{1,0:T(8,128)S(1)} %dynamic-slice_bitcast_fusion.2, pred[512,2048]{1,0:T(8,128)(4,1)} %fusion.120), kind=kLoop, calls=%fused_computation.20.clone.1 | loop fusion | flops 75497472 | bytes 126926848 | tf_op jit(solution)/shard_map/while/body/eval_jaxpr/convert_element_type | solution.py:190
  707.8 13.4 convolution_multiply_fusion.4
  721.2 15.5 %convolution_multiply_fusion.5 = f32[12,64,2048]{2,1,0:T(8,128)} fusion(bf16[512,12,64]{0,2,1:T(8,128)(2,1)} %bitcast.168, bf16[12,512,2048]{2,1,0:T(8,128)(2,1)} %multiply_convert_fusion.5), kind=kOutput, calls=%fused_computation.28.clone.1 | convolution fusion | flops 1612185600 | bytes 32243712 | tf_op jit(solution)/shard_map/while/body/eval_jaxpr/hqk,qhd->khd/dot_general | solution.py:201
  774.0 13.0 fusion.44
  787.2 88.8 %reduce-scatter.9.cloned.1.call-done = f32[2,512,768]{2,1,0:T(8,128)} async-done(((f32[2,2048,768]{2,1,0:T(8,128)}), f32[2,512,768]{2,1,0:T(8,128)}) %reduce-scatter.9.cloned.1.call-update) | async-done | bytes 3145744 | tf_op jit(solution)/shard_map/reduce_scatter | solution.py:223
  878.1 121.8 %reduce-scatter.7.cloned.1.call-done = f32[2,512,768]{2,1,0:T(8,128)} async-done(((f32[2,2048,768]{2,1,0:T(8,128)}), f32[2,512,768]{2,1,0:T(8,128)}) %reduce-scatter.7.cloned.1.call-update) | async-done | bytes 3145744 | tf_op jit(solution)/shard_map/reduce_scatter | solution.py:222
  1012.7 21.2 %reduce-scatter.15.cloned.1.call-done = f32[384,3072]{1,0:T(8,128)} async-done(((f32[768,3072]{1,0:T(8,128)}), f32[384,3072]{1,0:T(8,128)}) %reduce-scatter.15.cloned.1.call-update) | async-done | bytes 4718608 | tf_op jit(solution)/shard_map/reduce_scatter | solution.py:250
  1033.9 21.5 %reduce-scatter.17.cloned.1.call-done = f32[1536,768]{1,0:T(8,128)} async-done(((f32[3072,768]{1,0:T(8,128)}), f32[1536,768]{1,0:T(8,128)}) %reduce-scatter.17.cloned.1.call-update) | async-done | bytes 4718608 | tf_op jit(solution)/shard_map/reduce_scatter | solution.py:252
  1055.4 19.1 %reduce-scatter.11.cloned.1.call-done = f32[384,2304]{1,0:T(8,128)} async-done(((f32[768,2304]{1,0:T(8,128)}), f32[384,2304]{1,0:T(8,128)}) %reduce-scatter.11.cloned.1.call-update) | async-done | bytes 3538960 | tf_op jit(solution)/shard_map/reduce_scatter | solution.py:243
  1079.2 13.6 add_convert_fusion.2
  1108.0 82.4 %all-reduce.9 = (f32[384]{0:T(512)}, f32[384]{0:T(512)}, f32[384]{0:T(512)}, f32[384]{0:T(512)}, f32[384]{0:T(512)}, /*index=5*/f32[384]{0:T(512)}, f32[384]{0:T(512)}, f32[1536]{0:T(1024)}, f32[384]{0:T(512)}) all-reduce(f32[384]{0:T(512)S(1)} %dynamic-slice.11, ...), channel_id=1, replica_groups=mesh['cp'=4,'fsdp'=2,'rep'=4] {'cp','rep'}, use_global_device_ids=true, to_apply=%region_19.20 | all-reduce | flops 4608 | bytes 36864 | tf_op jit(solution)/shard_map/psum | solution.py:255
  1195.0 286.7 %all-reduce.14.cloned.1.call-done = (f32[384,2304]{1,0:T(8,128)}, f32[384,768]{1,0:T(8,128)}, f32[384,3072]{1,0:T(8,128)}, f32[1536,768]{1,0:T(8,128)}) async-done(((f32[384,2304]{1,0:T(8,128)}, f32[384,768]{1,0:T(8,128)}, f32[384,3072]{1,0:T(8,128)}, f32[1536,768]{1,0:T(8,128)}), (f32[384,2304]{1,0:T(8,128)}, f32[384,768]{1,0:T(8,128)}, f32[384,3072]{1,0:T(8,128)}, ...) | async-done | bytes 14155792 | tf_op jit(solution)/shard_map/psum | solution.py:255
  (311 shorter events, 227.7 us)
Async XLA Ops:
  7.2 17.8 %all-gather.16.cloned.1.call-start = ((), (), s32[]{:S(2)}) async-start(), calls=%async_computation.6 | async-start | bytes 5308416 | tf_op jit(solution)/shard_map/all_gather | solution.py:62
  7.9 98.5 %all-gather.20.cloned.1.call-start = ((), (), s32[]{:S(2)}) async-start(), calls=%async_computation.8 | async-start | bytes 7864320 | tf_op jit(solution)/shard_map/all_gather | solution.py:89
  10.6 20.4 %copy-start.30 = (f32[768]{0:T(1024)}, f32[768]{0:T(1024)S(1)}, u32[]{:S(2)}) copy-start(f32[768]{0:T(1024)S(1)} %reshape.445) | copy-start | bytes 9220
  35.1 143.8 %all-gather.18.cloned.1.call-start = ((), (), s32[]{:S(2)}) async-start(), calls=%async_computation.7 | async-start | bytes 7864320 | tf_op jit(solution)/shard_map/all_gather | solution.py:90
  36.8 297.3 %all-gather.22.cloned.1.call-start = ((), (), s32[]{:S(2)}) async-start(), calls=%async_computation.9 | async-start | bytes 1769472 | tf_op jit(solution)/shard_map/all_gather | solution.py:65
  37.4 141.6 %copy-start.23 = (s32[2,2048]{1,0:T(2,128)S(1)}, s32[2,2048]{1,0:T(2,128)}, u32[]{:S(2)}) copy-start(s32[2,2048]{1,0:T(2,128)} %param.21) | copy-start | bytes 49156
  37.4 301.1 %all-gather.24.cloned.1.call-start = ((), (), s32[]{:S(2)}) async-start(), calls=%async_computation.10 | async-start | bytes 7077888 | tf_op jit(solution)/shard_map/all_gather | solution.py:69
  38.0 311.6 %all-gather.26.cloned.1.call-start = ((), (), s32[]{:S(2)}) async-start(), calls=%async_computation.11 | async-start | bytes 7077888 | tf_op jit(solution)/shard_map/all_gather | solution.py:71
  38.5 837.5 %reduce-scatter.9.cloned.1.call-start = ((), (), s32[]{:S(2)}) async-start(), calls=%async_computation.13 | async-start | bytes 15728640 | tf_op jit(solution)/shard_map/reduce_scatter | solution.py:223
  178.9 155.2 %copy-start.46 = (f32[768]{0:T(1024)S(1)}, f32[768]{0:T(1024)}, u32[]{:S(2)}) copy-start(f32[768]{0:T(1024)} %reshape.447) | copy-start | bytes 9220
  212.5 24.5 %copy-start = (pred[512,2048]{1,0:T(8,128)(4,1)S(1)}, pred[512,2048]{1,0:T(8,128)(4,1)}, u32[]{:S(2)}) copy-start(pred[512,2048]{1,0:T(8,128)(4,1)} %fusion.105) | copy-start | bytes 3145732 | tf_op jit(solution)/shard_map/while
  212.5 24.5 %copy-start.3 = (bf16[1,2048,768]{1,2,0:T(8,128)(2,1)S(1)}, bf16[1,2048,768]{1,2,0:T(8,128)(2,1)}, u32[]{:S(2)}) copy-start(bf16[1,2048,768]{1,2,0:T(8,128)(2,1)} %get-tuple-element.681) | copy-start | bytes 9437188 | tf_op jit(solution)/shard_map/while
  289.6 22.9 %copy-start = (pred[512,2048]{1,0:T(8,128)(4,1)S(1)}, pred[512,2048]{1,0:T(8,128)(4,1)}, u32[]{:S(2)}) copy-start(pred[512,2048]{1,0:T(8,128)(4,1)} %fusion.105) | copy-start | bytes 3145732 | tf_op jit(solution)/shard_map/while
  289.6 22.9 %copy-start.3 = (bf16[1,2048,768]{1,2,0:T(8,128)(2,1)S(1)}, bf16[1,2048,768]{1,2,0:T(8,128)(2,1)}, u32[]{:S(2)}) copy-start(bf16[1,2048,768]{1,2,0:T(8,128)(2,1)} %get-tuple-element.681) | copy-start | bytes 9437188 | tf_op jit(solution)/shard_map/while
  337.9 36.6 %copy-start.6 = (f32[1024,768]{1,0:T(8,128)}, f32[1024,768]{1,0:T(8,128)S(1)}, u32[]{:S(2)}) copy-start(f32[1024,768]{1,0:T(8,128)S(1)} %get-tuple-element.552) | copy-start | bytes 9437188
  338.0 36.6 %copy-start.24 = (f32[1024]{0:T(1024)}, f32[1024]{0:T(1024)S(1)}, u32[]{:S(2)}) copy-start(f32[1024]{0:T(1024)S(1)} %broadcast_multiply_fusion) | copy-start | bytes 12292
  338.5 36.1 %copy-start.26 = (f32[1024]{0:T(1024)}, f32[1024]{0:T(1024)S(1)}, u32[]{:S(2)}) copy-start(f32[1024]{0:T(1024)S(1)} %fusion.36) | copy-start | bytes 12292
  349.5 18.8 %copy-start.54 = (bf16[768,3072]{1,0:T(8,128)(2,1)S(1)}, bf16[768,3072]{1,0:T(8,128)(2,1)}, u32[]{:S(2)}) copy-start(bf16[768,3072]{1,0:T(8,128)(2,1)} %all-gather.24.cloned.1.call-done) | copy-start | bytes 14155780
  755.1 244.8 %reduce-scatter.7.cloned.1.call-start = ((), (), s32[]{:S(2)}) async-start(), calls=%async_computation.12 | async-start | bytes 15728640 | tf_op jit(solution)/shard_map/reduce_scatter | solution.py:222
  755.9 256.8 %reduce-scatter.13.cloned.1.call-start = ((), (), s32[]{:S(2)}) async-start(), calls=%async_computation.15 | async-start | bytes 3538944 | tf_op jit(solution)/shard_map/reduce_scatter | solution.py:246
  760.9 273.0 %reduce-scatter.15.cloned.1.call-start = ((), (), s32[]{:S(2)}) async-start(), calls=%async_computation.16 | async-start | bytes 14155776 | tf_op jit(solution)/shard_map/reduce_scatter | solution.py:250
  772.6 282.7 %reduce-scatter.17.cloned.1.call-start = ((), (), s32[]{:S(2)}) async-start(), calls=%async_computation.17 | async-start | bytes 14155776 | tf_op jit(solution)/shard_map/reduce_scatter | solution.py:252
  787.0 287.5 %reduce-scatter.11.cloned.1.call-start = ((), (), s32[]{:S(2)}) async-start(), calls=%async_computation.14 | async-start | bytes 10616832 | tf_op jit(solution)/shard_map/reduce_scatter | solution.py:243
  878.1 133.4 %copy-start.15 = (bf16[2,512,768]{2,1,0:T(8,128)(2,1)}, bf16[2,512,768]{2,1,0:T(8,128)(2,1)S(1)}, u32[]{:S(2)}) copy-start(bf16[2,512,768]{2,1,0:T(8,128)(2,1)S(1)} %convert.15) | copy-start | bytes 4718596
  1011.5 470.1 %all-reduce.14.cloned.1.call-start = ((), (), s32[]{:S(2)}) async-start(), calls=%async_computation.18 | async-start | bytes 28311552 | tf_op jit(solution)/shard_map/psum | solution.py:255
  1079.2 13.6 copy-start.5
  1079.2 13.6 copy-start.16
  1079.2 13.6 copy-start.18
  1079.2 13.6 copy-start.31
  1079.2 13.6 copy-start.35
  1079.2 13.6 copy-start.55
  1101.7 88.7 %copy-start.39 = (f32[1024]{0:T(1024)S(1)}, f32[1024]{0:T(1024)}, u32[]{:S(2)}) copy-start(f32[1024]{0:T(1024)} %copy-done.38) | copy-start | bytes 12292
  (49 other events, 226.4 us)
Sparse Core Ops, SparseCore 0:
  9.6 15.3 all-gather.15
  35.2 71.1 all-gather.19
  108.9 70.0 all-gather.17
  180.3 9.2 all-gather.21
  191.0 15.5 all-gather.23
  208.0 15.6 all-gather.25
  755.2 120.7 reduce-scatter.8
  879.2 120.7 reduce-scatter.6
  1002.8 9.8 reduce-scatter.12
  1014.9 18.9 reduce-scatter.14
  1036.3 19.0 reduce-scatter.16
  1057.7 16.8 reduce-scatter.10
  1081.0 400.6 all-reduce.13
where the time goes:
time: 1500 us
  waiting for transfers between devices  695 us (46%)
  matrix products  410 us (27%)
  other arithmetic  160 us (11%)
  local copies, waits for them, and re-layouts  111 us (7%)
  blocking collectives  103 us (7%)
  between operations  16.3 us (1%)
    psum x1, waiting for transfers between devices, body(): lax.psum((shards[0], shards[1], shards[2], shards[3], shards[4], shards[5...  287 us
    reduce_scatter x1, waiting for transfers between devices, body(): lax.psum_scatter(d_key_all, 'cp', scatter_dimension=1, tiled=True)  122 us
    reduce_scatter x1, waiting for transfers between devices, body(): lax.psum_scatter(d_value_all, 'cp', scatter_dimension=1, tiled=True)  88.8 us
    dot_general x4, matrix products, masked_scores(): jnp.einsum('qhd,khd->hqk', q_three, k_three, preferred_element_type=jnp.f...  86.3 us
    convert_element_type x2, other arithmetic, attend_back(): d_scores = (probs * (d_probs - delta)).astype(jnp.bfloat16)  82.8 us
    psum x1, blocking collectives, body(): lax.psum((shards[0], shards[1], shards[2], shards[3], shards[4], shards[5...  82.4 us
    dot_general x2, matrix products, attend_back(): jnp.einsum('qhd,khd->hqk', d_three, v_three, preferred_element_type=jnp.f...  75.1 us
    all_gather x1, waiting for transfers between devices, body(): lax.all_gather(value_loc, 'cp', axis=1, tiled=True)  72.5 us
  transfers between devices with their start and end apart: 13, of which 10 were waited for; matrix products, arithmetic and copies ran while one was open for 17% of the time, Pallas kernels for 0%

commit v1 on v0

--- a/solution.py
+++ b/solution.py
@@ -86,7 +86,9 @@
     key_loc = merged[:, :, width : 2 * width]
     value_loc = merged[:, :, 2 * width :]
     keys_all, values_all = (
-        lax.all_gather(key_loc, "cp", axis=1, tiled=True),
+        jnp.concatenate(
+            lax.all_to_all(jnp.stack([key_loc] * lax.axis_size("cp")), "cp", 0, 0), axis=1
+        ),
         lax.all_gather(value_loc, "cp", axis=1, tiled=True),
     )
     key_pos = jnp.arange(seq_len)

time: 1500 us -> 1510 us (level)
  waiting for transfers between devices: 695 us -> 666 us
  local copies, waits for them, and re-layouts: 111 us -> 135 us
    all_to_all x0 -> x1, waiting for transfers between devices: none -> 86.2 us  [body(): lax.all_to_all(jnp.stack([key_loc] * lax.axis_size('cp')), 'cp', 0, 0)]
    all_gather x1, waiting for transfers between devices: 72.5 us -> 12.3 us  [body(): lax.all_gather(value_loc, 'cp', axis=1, tiled=True)]
    all_gather x1, waiting for transfers between devices: 56.1 us -> 0.02 us  [body(): lax.all_gather(key_loc, 'cp', axis=1, tiled=True)]
    dynamic_slice x18 -> x22, local copies, waits for them, and re-layouts: 30 us -> 41.3 us  [body(): lax.map(attend, (query, keys_all, values_all, segments, segments))]
  transfers between devices with their start and end apart: 13 -> 14, of which waited for: 10 -> 10; matrix products, arithmetic and copies ran while one was open for 17% -> 20% of each run, Pallas kernels for 0% -> 0%
where the time goes in v1:
time: 1510 us; the launch traced here: 1500 us
  waiting for transfers between devices  666 us (44%)
  matrix products  411 us (27%)
  other arithmetic  159 us (11%)
  local copies, waits for them, and re-layouts  135 us (9%)
  blocking collectives  102 us (7%)
  between operations  16.3 us (1%)
    psum x1, waiting for transfers between devices, body(): lax.psum((shards[0], shards[1], shards[2], shards[3], shards[4], shards[5...  287 us
    reduce_scatter x1, waiting for transfers between devices, body(): lax.psum_scatter(d_key_all, 'cp', scatter_dimension=1, tiled=True)  122 us
    reduce_scatter x1, waiting for transfers between devices, body(): lax.psum_scatter(d_value_all, 'cp', scatter_dimension=1, tiled=True)  89.2 us
    dot_general x4, matrix products, masked_scores(): jnp.einsum('qhd,khd->hqk', q_three, k_three, preferred_element_type=jnp.f...  86.9 us
    all_to_all x1, waiting for transfers between devices, body(): lax.all_to_all(jnp.stack([key_loc] * lax.axis_size('cp')), 'cp', 0, 0)  86.2 us
    convert_element_type x2, other arithmetic, attend_back(): d_scores = (probs * (d_probs - delta)).astype(jnp.bfloat16)  82.9 us
    psum x1, blocking collectives, body(): lax.psum((shards[0], shards[1], shards[2], shards[3], shards[4], shards[5...  82.5 us
    dot_general x2, matrix products, attend_back(): jnp.einsum('qhd,khd->hqk', d_three, v_three, preferred_element_type=jnp.f...  75.2 us
  transfers between devices with their start and end apart: 14, of which 10 were waited for; matrix products, arithmetic and copies ran while one was open for 20% of the time, Pallas kernels for 0%

profile of v1, /device:TPU:0, one launch (start us, length us, event | category | flops | bytes accessed | tf_op | source)
XLA Modules:
  0.0 1498.2 jit_solution(17773981939482871922)
XLA Ops:
  58.1 86.2 %all-to-all-done = bf16[4,2,512,768]{2,3,1,0:T(8,128)(2,1)} async-done(((bf16[4,2,512,768]{2,3,1,0:T(8,128)(2,1)}), bf16[4,2,512,768]{2,3,1,0:T(8,128)(2,1)}, u32[]{:S(2)}, u32[]{:S(2)}) %all-to-all-start) | async-done | bytes 6291488 | tf_op jit(solution)/shard_map/all_to_all | solution.py:90
  152.9 12.3 all-gather.18.cloned.1.call-done
  165.3 166.8 %while.34 = (s32[]{:T(128)}, bf16[2,512,768]{2,1,0:T(8,128)(2,1)}, f32[2,12,512]{2,1,0:T(8,128)S(1)}, bf16[2,2048,768]{1,2,0:T(8,128)(2,1)}, s32[2,2048]{1,0:T(2...) while((s32[]{:T(128)}, bf16[2,512,768]{2,1,0:T(8,128)(2,1)}, ...), condition=%wide.region_5.6_spmd.clone, body=%wide.region_2.5_spmd.clone.sunk | while | flops 3375753728 | bytes 203679984 | solution.py:129
  181.1 24.5 %fusion.106 = (f32[12,512]{1,0:T(8,128)S(1)}, f32[12,512,2048]{2,1,0:T(8,128)}) fusion(pred[512,2048]{1,0:T(8,128)(4,1)} %fusion.105, bf16[512,12,64]{0,2,1:T(8,128)(2,1)} %bitcast.173, bf16[2048,12,64]{0,2,1:T(8,128)(2,1)S(1)} %bitcast.168), kind=kOutput, calls=%fused_computation.5.clone.1 | convolution fusion | flops 1648355328 | bytes 55336960 | tf_op jit(solution)/shard_map/while/body/eval_jaxpr/qhd,khd->hqk/dot_general | solution.py:101
  205.6 23.9 %fusion.107 = f32[12,512]{1,0:T(8,128)S(1)} fusion(f32[12,512,2048]{2,1,0:T(8,128)} %get-tuple-element.698, f32[12,512]{1,0:T(8,128)S(1)} %get-tuple-element.699, pred[512,2048]{1,0:T(8,128)(4,1)} %fusion.105), kind=kLoop, calls=%fused_computation.6.clone.1 | loop fusion | flops 50325504 | bytes 51429376 | tf_op jit(solution)/shard_map/while/body/eval_jaxpr/reduce_sum | solution.py:116
  229.5 20.2 %fusion.108 = bf16[12,64,512]{2,1,0:T(8,128)(2,1)S(1)} fusion(bf16[2048,12,64]{0,2,1:T(8,128)(2,1)S(1)} %bitcast.177, f32[12,512,2048]{2,1,0:T(8,128)} %get-tuple-element.698, f32[12,512]{1,0:T(8,128)S(1)} %fusion.107, f32[12,512]{1,0:T(8,128)S(1)} %get-tuple-element.699, pred[512,2048]{1,0:T(8,128)(4,1)S(1)} %copy-done), kind=kOutput, calls=%fused_computation.10.clone.1 | convolution fusion | flops 1673920512 | bytes 55361536 | tf_op jit(solution)/shard_map/while/body/eval_jaxpr/hqk,khd->qhd/dot_general | solution.py:118
  266.2 21.5 %fusion.106 = (f32[12,512]{1,0:T(8,128)S(1)}, f32[12,512,2048]{2,1,0:T(8,128)}) fusion(pred[512,2048]{1,0:T(8,128)(4,1)} %fusion.105, bf16[512,12,64]{0,2,1:T(8,128)(2,1)} %bitcast.173, bf16[2048,12,64]{0,2,1:T(8,128)(2,1)S(1)} %bitcast.168), kind=kOutput, calls=%fused_computation.5.clone.1 | convolution fusion | flops 1648355328 | bytes 55336960 | tf_op jit(solution)/shard_map/while/body/eval_jaxpr/qhd,khd->hqk/dot_general | solution.py:101
  287.7 22.8 %fusion.107 = f32[12,512]{1,0:T(8,128)S(1)} fusion(f32[12,512,2048]{2,1,0:T(8,128)} %get-tuple-element.698, f32[12,512]{1,0:T(8,128)S(1)} %get-tuple-element.699, pred[512,2048]{1,0:T(8,128)(4,1)} %fusion.105), kind=kLoop, calls=%fused_computation.6.clone.1 | loop fusion | flops 50325504 | bytes 51429376 | tf_op jit(solution)/shard_map/while/body/eval_jaxpr/reduce_sum | solution.py:116
  310.5 20.2 %fusion.108 = bf16[12,64,512]{2,1,0:T(8,128)(2,1)S(1)} fusion(bf16[2048,12,64]{0,2,1:T(8,128)(2,1)S(1)} %bitcast.177, f32[12,512,2048]{2,1,0:T(8,128)} %get-tuple-element.698, f32[12,512]{1,0:T(8,128)S(1)} %fusion.107, f32[12,512]{1,0:T(8,128)S(1)} %get-tuple-element.699, pred[512,2048]{1,0:T(8,128)(4,1)S(1)} %copy-done), kind=kOutput, calls=%fused_computation.10.clone.1 | convolution fusion | flops 1673920512 | bytes 55361536 | tf_op jit(solution)/shard_map/while/body/eval_jaxpr/hqk,khd->qhd/dot_general | solution.py:118
  347.5 18.8 %convert_reduce_fusion = (f32[3072]{0:T(1024)}, bf16[1024,3072]{1,0:T(8,128)(2,1)S(1)}) fusion(bf16[1024,768]{1,0:T(8,128)(2,1)} %bitcast.180, bf16[3072,768]{1,0:T(8,128)(2,1)} %all-gather.24.cloned.1.call-done, f32[1024,3072]{1,0:T(8,128)} %fusion.43, f32[3072]{0:T(1024)S(1)} %bitcast.205), kind=kOutput, calls=%fused_computation.52 | convolution fusion | flops 4916769792 | bytes 25190400 | tf_op jit(solution)/shard_map/dot_general | solution.py:30
  379.4 373.9 %while.35 = (s32[]{:T(128)}, bf16[2,512,768]{2,1,0:T(8,128)(2,1)}, f32[2,2048,768]{2,1,0:T(8,128)}, f32[2,2048,768]{2,1,0:T(8,128)}, bf16[2,2048,768]{1,2,0:T(8,...) while((s32[]{:T(128)}, bf16[2,512,768]{2,1,0:T(8,128)(2,1)}, ...), condition=%wide.region_12.13_spmd.clone, body=%wide.region_10.12_spmd.clone.sunk | while | flops 8247306752 | bytes 519514368 | solution.py:220
  390.5 20.5 %fusion.119 = f32[12,512,2048]{2,1,0:T(8,128)} fusion(bf16[512,12,64]{0,2,1:T(8,128)(2,1)} %bitcast.170, bf16[2048,12,64]{0,2,1:T(8,128)(2,1)S(1)} %bitcast.165), kind=kOutput, calls=%fused_computation.114.clone.1 | convolution fusion | flops 1610612736 | bytes 54263808 | tf_op jit(solution)/shard_map/while/body/eval_jaxpr/qhd,khd->hqk/dot_general | solution.py:101
  411.0 23.1 %fusion.121 = f32[12,64,2048]{2,1,0:T(8,128)} fusion(bf16[512,12,64]{0,2,1:T(8,128)(2,1)} %bitcast.175, f32[12,512,2048]{2,1,0:T(8,128)} %fusion.119, f32[12,512]{1,0:T(8,128)S(1)} %dynamic-slice_bitcast_fusion.2, pred[512,2048]{1,0:T(8,128)(4,1)} %fusion.120), kind=kOutput, calls=%fused_computation.24.clone.1 | convolution fusion | flops 1660944384 | bytes 58482688 | tf_op jit(solution)/shard_map/while/body/eval_jaxpr/hqk,qhd->khd/dot_general | solution.py:211
  440.8 37.6 %multiply_reduce_fusion.5 = (f32[12,512]{1,0:T(8,128)S(1)}, f32[12,512,2048]{2,1,0:T(8,128)}) fusion(f32[12,512,2048]{2,1,0:T(8,128)} %fusion.119, f32[12,512]{1,0:T(8,128)S(1)} %dynamic-slice_bitcast_fusion.2, pred[512,2048]{1,0:T(8,128)(4,1)} %fusion.120, bf16[512,12,64]{0,2,1:T(8,128)(2,1)} %bitcast.176, bf16[2048,12,64]{0,2,1:T(8,128)(2,1)} %bitcast.169), kind=kOutput, calls=%fused_computation.21.clone.1 | convolution fusion | flops 1673521152 | bytes 105693184 | tf_op jit(solution)/shard_map/while/body/eval_jaxpr/qhd,khd->hqk/dot_general | solution.py:190
  478.4 41.4 %multiply_convert_fusion.5 = bf16[12,512,2048]{2,1,0:T(8,128)(2,1)} fusion(f32[12,512,2048]{2,1,0:T(8,128)} %get-tuple-element.712, f32[12,512,2048]{2,1,0:T(8,128)} %fusion.119, f32[12,512]{1,0:T(8,128)S(1)} %get-tuple-element.713, f32[12,512]{1,0:T(8,128)S(1)} %dynamic-slice_bitcast_fusion.2, pred[512,2048]{1,0:T(8,128)(4,1)} %fusion.120), kind=kLoop, calls=%fused_computation.20.clone.1 | loop fusion | flops 75497472 | bytes 126926848 | tf_op jit(solution)/shard_map/while/body/eval_jaxpr/convert_element_type | solution.py:192
  519.8 13.4 convolution_multiply_fusion.4
  533.2 15.5 %convolution_multiply_fusion.5 = f32[12,64,2048]{2,1,0:T(8,128)} fusion(bf16[512,12,64]{0,2,1:T(8,128)(2,1)} %bitcast.171, bf16[12,512,2048]{2,1,0:T(8,128)(2,1)} %multiply_convert_fusion.5), kind=kOutput, calls=%fused_computation.28.clone.1 | convolution fusion | flops 1612185600 | bytes 32243712 | tf_op jit(solution)/shard_map/while/body/eval_jaxpr/hqk,qhd->khd/dot_general | solution.py:203
  576.8 20.5 %fusion.119 = f32[12,512,2048]{2,1,0:T(8,128)} fusion(bf16[512,12,64]{0,2,1:T(8,128)(2,1)} %bitcast.170, bf16[2048,12,64]{0,2,1:T(8,128)(2,1)S(1)} %bitcast.165), kind=kOutput, calls=%fused_computation.114.clone.1 | convolution fusion | flops 1610612736 | bytes 54263808 | tf_op jit(solution)/shard_map/while/body/eval_jaxpr/qhd,khd->hqk/dot_general | solution.py:101
  597.2 23.1 %fusion.121 = f32[12,64,2048]{2,1,0:T(8,128)} fusion(bf16[512,12,64]{0,2,1:T(8,128)(2,1)} %bitcast.175, f32[12,512,2048]{2,1,0:T(8,128)} %fusion.119, f32[12,512]{1,0:T(8,128)S(1)} %dynamic-slice_bitcast_fusion.2, pred[512,2048]{1,0:T(8,128)(4,1)} %fusion.120), kind=kOutput, calls=%fused_computation.24.clone.1 | convolution fusion | flops 1660944384 | bytes 58482688 | tf_op jit(solution)/shard_map/while/body/eval_jaxpr/hqk,qhd->khd/dot_general | solution.py:211
  627.0 37.6 %multiply_reduce_fusion.5 = (f32[12,512]{1,0:T(8,128)S(1)}, f32[12,512,2048]{2,1,0:T(8,128)}) fusion(f32[12,512,2048]{2,1,0:T(8,128)} %fusion.119, f32[12,512]{1,0:T(8,128)S(1)} %dynamic-slice_bitcast_fusion.2, pred[512,2048]{1,0:T(8,128)(4,1)} %fusion.120, bf16[512,12,64]{0,2,1:T(8,128)(2,1)} %bitcast.176, bf16[2048,12,64]{0,2,1:T(8,128)(2,1)} %bitcast.169), kind=kOutput, calls=%fused_computation.21.clone.1 | convolution fusion | flops 1673521152 | bytes 105693184 | tf_op jit(solution)/shard_map/while/body/eval_jaxpr/qhd,khd->hqk/dot_general | solution.py:190
  664.6 41.4 %multiply_convert_fusion.5 = bf16[12,512,2048]{2,1,0:T(8,128)(2,1)} fusion(f32[12,512,2048]{2,1,0:T(8,128)} %get-tuple-element.712, f32[12,512,2048]{2,1,0:T(8,128)} %fusion.119, f32[12,512]{1,0:T(8,128)S(1)} %get-tuple-element.713, f32[12,512]{1,0:T(8,128)S(1)} %dynamic-slice_bitcast_fusion.2, pred[512,2048]{1,0:T(8,128)(4,1)} %fusion.120), kind=kLoop, calls=%fused_computation.20.clone.1 | loop fusion | flops 75497472 | bytes 126926848 | tf_op jit(solution)/shard_map/while/body/eval_jaxpr/convert_element_type | solution.py:192
  706.0 13.4 convolution_multiply_fusion.4
  719.4 15.5 %convolution_multiply_fusion.5 = f32[12,64,2048]{2,1,0:T(8,128)} fusion(bf16[512,12,64]{0,2,1:T(8,128)(2,1)} %bitcast.171, bf16[12,512,2048]{2,1,0:T(8,128)(2,1)} %multiply_convert_fusion.5), kind=kOutput, calls=%fused_computation.28.clone.1 | convolution fusion | flops 1612185600 | bytes 32243712 | tf_op jit(solution)/shard_map/while/body/eval_jaxpr/hqk,qhd->khd/dot_general | solution.py:203
  772.3 13.2 fusion.44
  785.8 89.2 %reduce-scatter.9.cloned.1.call-done = f32[2,512,768]{2,1,0:T(8,128)} async-done(((f32[2,2048,768]{2,1,0:T(8,128)}), f32[2,512,768]{2,1,0:T(8,128)}) %reduce-scatter.9.cloned.1.call-update) | async-done | bytes 3145744 | tf_op jit(solution)/shard_map/reduce_scatter | solution.py:225
  877.1 121.8 %reduce-scatter.7.cloned.1.call-done = f32[2,512,768]{2,1,0:T(8,128)} async-done(((f32[2,2048,768]{2,1,0:T(8,128)}), f32[2,512,768]{2,1,0:T(8,128)}) %reduce-scatter.7.cloned.1.call-update) | async-done | bytes 3145744 | tf_op jit(solution)/shard_map/reduce_scatter | solution.py:224
  1011.6 21.2 %reduce-scatter.15.cloned.1.call-done = f32[384,3072]{1,0:T(8,128)} async-done(((f32[768,3072]{1,0:T(8,128)}), f32[384,3072]{1,0:T(8,128)}) %reduce-scatter.15.cloned.1.call-update) | async-done | bytes 4718608 | tf_op jit(solution)/shard_map/reduce_scatter | solution.py:252
  1032.8 21.5 %reduce-scatter.17.cloned.1.call-done = f32[1536,768]{1,0:T(8,128)} async-done(((f32[3072,768]{1,0:T(8,128)}), f32[1536,768]{1,0:T(8,128)}) %reduce-scatter.17.cloned.1.call-update) | async-done | bytes 4718608 | tf_op jit(solution)/shard_map/reduce_scatter | solution.py:254
  1054.3 19.1 %reduce-scatter.11.cloned.1.call-done = f32[384,2304]{1,0:T(8,128)} async-done(((f32[768,2304]{1,0:T(8,128)}), f32[384,2304]{1,0:T(8,128)}) %reduce-scatter.11.cloned.1.call-update) | async-done | bytes 3538960 | tf_op jit(solution)/shard_map/reduce_scatter | solution.py:245
  1078.2 13.6 add_convert_fusion.2
  1106.9 82.5 %all-reduce.9 = (f32[384]{0:T(512)}, f32[384]{0:T(512)}, f32[384]{0:T(512)}, f32[384]{0:T(512)}, f32[384]{0:T(512)}, /*index=5*/f32[384]{0:T(512)}, f32[384]{0:T(512)}, f32[1536]{0:T(1024)}, f32[384]{0:T(512)}) all-reduce(f32[384]{0:T(512)S(1)} %dynamic-slice.11, ...), channel_id=1, replica_groups=mesh['cp'=4,'fsdp'=2,'rep'=4] {'cp','rep'}, use_global_device_ids=true, to_apply=%region_19.20 | all-reduce | flops 4608 | bytes 36864 | tf_op jit(solution)/shard_map/psum | solution.py:257
  1194.0 286.6 %all-reduce.14.cloned.1.call-done = (f32[384,2304]{1,0:T(8,128)}, f32[384,768]{1,0:T(8,128)}, f32[384,3072]{1,0:T(8,128)}, f32[1536,768]{1,0:T(8,128)}) async-done(((f32[384,2304]{1,0:T(8,128)}, f32[384,768]{1,0:T(8,128)}, f32[384,3072]{1,0:T(8,128)}, f32[1536,768]{1,0:T(8,128)}), (f32[384,2304]{1,0:T(8,128)}, f32[384,768]{1,0:T(8,128)}, f32[384,3072]{1,0:T(8,128)}, ...) | async-done | bytes 14155792 | tf_op jit(solution)/shard_map/psum | solution.py:257
  (321 shorter events, 257.2 us)
Async XLA Ops:
  7.2 17.8 %all-gather.16.cloned.1.call-start = ((), (), s32[]{:S(2)}) async-start(), calls=%async_computation.7 | async-start | bytes 5308416 | tf_op jit(solution)/shard_map/all_gather | solution.py:62
  7.9 157.3 %all-gather.18.cloned.1.call-start = ((), (), s32[]{:S(2)}) async-start(), calls=%async_computation.8 | async-start | bytes 7864320 | tf_op jit(solution)/shard_map/all_gather | solution.py:92
  10.6 20.4 %copy-start.31 = (f32[768]{0:T(1024)}, f32[768]{0:T(1024)S(1)}, u32[]{:S(2)}) copy-start(f32[768]{0:T(1024)S(1)} %reshape.455) | copy-start | bytes 9220
  34.1 298.0 %all-gather.20.cloned.1.call-start = ((), (), s32[]{:S(2)}) async-start(), calls=%async_computation.9 | async-start | bytes 1769472 | tf_op jit(solution)/shard_map/all_gather | solution.py:65
  34.8 301.7 %all-gather.22.cloned.1.call-start = ((), (), s32[]{:S(2)}) async-start(), calls=%async_computation.10 | async-start | bytes 7077888 | tf_op jit(solution)/shard_map/all_gather | solution.py:69
  35.4 312.1 %all-gather.24.cloned.1.call-start = ((), (), s32[]{:S(2)}) async-start(), calls=%async_computation.11 | async-start | bytes 7077888 | tf_op jit(solution)/shard_map/all_gather | solution.py:71
  41.0 103.3 %all-to-all-start = ((bf16[4,2,512,768]{2,3,1,0:T(8,128)(2,1)}), bf16[4,2,512,768]{2,3,1,0:T(8,128)(2,1)}, u32[]{:S(2)}, u32[]{:S(2)}) async-start(bf16[4,2,512,768]{2,3,1,0:T(8,128)(2,1)} %stack.2), calls=%async_computation | async-start | bytes 12582912 | tf_op jit(solution)/shard_map/all_to_all | solution.py:90
  46.6 332.8 %all-gather.26.cloned.1.call-start = ((), (), s32[]{:S(2)}) async-start(), calls=%async_computation.12 | async-start | bytes 7864320 | tf_op jit(solution)/shard_map/all_gather | solution.py:160
  56.4 818.6 %reduce-scatter.9.cloned.1.call-start = ((), (), s32[]{:S(2)}) async-start(), calls=%async_computation.14 | async-start | bytes 15728640 | tf_op jit(solution)/shard_map/reduce_scatter | solution.py:225
  58.1 107.2 %copy-start.24 = (s32[2,2048]{1,0:T(2,128)S(1)}, s32[2,2048]{1,0:T(2,128)}, u32[]{:S(2)}) copy-start(s32[2,2048]{1,0:T(2,128)} %param.21) | copy-start | bytes 49156
  165.3 166.9 %copy-start.47 = (f32[768]{0:T(1024)S(1)}, f32[768]{0:T(1024)}, u32[]{:S(2)}) copy-start(f32[768]{0:T(1024)} %reshape.457) | copy-start | bytes 9220
  205.6 23.9 %copy-start = (pred[512,2048]{1,0:T(8,128)(4,1)S(1)}, pred[512,2048]{1,0:T(8,128)(4,1)}, u32[]{:S(2)}) copy-start(pred[512,2048]{1,0:T(8,128)(4,1)} %fusion.105) | copy-start | bytes 3145732 | tf_op jit(solution)/shard_map/while
  205.6 23.9 %copy-start.2 = (bf16[1,2048,768]{1,2,0:T(8,128)(2,1)S(1)}, bf16[1,2048,768]{1,2,0:T(8,128)(2,1)}, u32[]{:S(2)}) copy-start(bf16[1,2048,768]{1,2,0:T(8,128)(2,1)} %constant_dynamic-slice_fusion.18) | copy-start | bytes 9437188 | tf_op jit(solution)/shard_map/while
  287.7 22.8 %copy-start = (pred[512,2048]{1,0:T(8,128)(4,1)S(1)}, pred[512,2048]{1,0:T(8,128)(4,1)}, u32[]{:S(2)}) copy-start(pred[512,2048]{1,0:T(8,128)(4,1)} %fusion.105) | copy-start | bytes 3145732 | tf_op jit(solution)/shard_map/while
  287.7 22.8 %copy-start.2 = (bf16[1,2048,768]{1,2,0:T(8,128)(2,1)S(1)}, bf16[1,2048,768]{1,2,0:T(8,128)(2,1)}, u32[]{:S(2)}) copy-start(bf16[1,2048,768]{1,2,0:T(8,128)(2,1)} %constant_dynamic-slice_fusion.18) | copy-start | bytes 9437188 | tf_op jit(solution)/shard_map/while
  335.9 36.6 %copy-start.6 = (f32[1024,768]{1,0:T(8,128)}, f32[1024,768]{1,0:T(8,128)S(1)}, u32[]{:S(2)}) copy-start(f32[1024,768]{1,0:T(8,128)S(1)} %get-tuple-element.571) | copy-start | bytes 9437188
  336.0 36.6 %copy-start.25 = (f32[1024]{0:T(1024)}, f32[1024]{0:T(1024)S(1)}, u32[]{:S(2)}) copy-start(f32[1024]{0:T(1024)S(1)} %broadcast_multiply_fusion) | copy-start | bytes 12292
  336.5 36.1 %copy-start.27 = (f32[1024]{0:T(1024)}, f32[1024]{0:T(1024)S(1)}, u32[]{:S(2)}) copy-start(f32[1024]{0:T(1024)S(1)} %fusion.36) | copy-start | bytes 12292
  347.5 18.9 %copy-start.55 = (bf16[768,3072]{1,0:T(8,128)(2,1)S(1)}, bf16[768,3072]{1,0:T(8,128)(2,1)}, u32[]{:S(2)}) copy-start(bf16[768,3072]{1,0:T(8,128)(2,1)} %all-gather.22.cloned.1.call-done) | copy-start | bytes 14155780
  753.4 245.5 %reduce-scatter.7.cloned.1.call-start = ((), (), s32[]{:S(2)}) async-start(), calls=%async_computation.13 | async-start | bytes 15728640 | tf_op jit(solution)/shard_map/reduce_scatter | solution.py:224
  754.2 257.4 %reduce-scatter.13.cloned.1.call-start = ((), (), s32[]{:S(2)}) async-start(), calls=%async_computation.16 | async-start | bytes 3538944 | tf_op jit(solution)/shard_map/reduce_scatter | solution.py:248
  759.1 273.7 %reduce-scatter.15.cloned.1.call-start = ((), (), s32[]{:S(2)}) async-start(), calls=%async_computation.17 | async-start | bytes 14155776 | tf_op jit(solution)/shard_map/reduce_scatter | solution.py:252
  770.9 283.4 %reduce-scatter.17.cloned.1.call-start = ((), (), s32[]{:S(2)}) async-start(), calls=%async_computation.18 | async-start | bytes 14155776 | tf_op jit(solution)/shard_map/reduce_scatter | solution.py:254
  785.5 287.9 %reduce-scatter.11.cloned.1.call-start = ((), (), s32[]{:S(2)}) async-start(), calls=%async_computation.15 | async-start | bytes 10616832 | tf_op jit(solution)/shard_map/reduce_scatter | solution.py:245
  877.0 133.4 %copy-start.16 = (bf16[2,512,768]{2,1,0:T(8,128)(2,1)}, bf16[2,512,768]{2,1,0:T(8,128)(2,1)S(1)}, u32[]{:S(2)}) copy-start(bf16[2,512,768]{2,1,0:T(8,128)(2,1)S(1)} %convert.15) | copy-start | bytes 4718596
  1010.5 470.1 %all-reduce.14.cloned.1.call-start = ((), (), s32[]{:S(2)}) async-start(), calls=%async_computation.19 | async-start | bytes 28311552 | tf_op jit(solution)/shard_map/psum | solution.py:257
  1078.1 13.6 copy-start.5
  1078.1 13.6 copy-start.17
  1078.1 13.6 copy-start.19
  1078.1 13.6 copy-start.32
  1078.1 13.6 copy-start.36
  1100.6 88.8 %copy-start.40 = (f32[1024]{0:T(1024)S(1)}, f32[1024]{0:T(1024)}, u32[]{:S(2)}) copy-start(f32[1024]{0:T(1024)} %copy-done.39) | copy-start | bytes 12292
  (51 other events, 258.3 us)
Sparse Core Ops, SparseCore 0:
  9.6 15.3 all-gather.15
  34.2 130.9 all-gather.17
  166.8 9.2 all-gather.19
  177.5 15.5 all-gather.21
  194.5 15.6 all-gather.23
  212.4 71.1 all-gather.25
  753.5 121.4 reduce-scatter.8
  878.1 120.7 reduce-scatter.6
  1001.7 9.8 reduce-scatter.12
  1013.8 18.9 reduce-scatter.14
  1035.2 19.0 reduce-scatter.16
  1056.6 16.8 reduce-scatter.10
  1079.9 400.6 all-reduce.13
